TPU v7x, 32 devices: a whole 2x2x4 slice. The times are simulated.
32 devices in a mesh: dp: 4 (over y, x), seq: 8 (over z, core).
Axes of the slice: x: 2, y: 2, z: 4, core: 2. Of those that a mesh axis runs over, the one named last changes fastest.
Arguments:
- hidden: float32 [4, 2048, 768], P('dp', 'seq'), may hold values from -6 to 6
- cotangent: float32 [4, 2048, 768], P('dp', 'seq'), may hold values from -6 to 6
- lengths: int32 [4], P('dp'), may hold values from 1024 to 2048, as said below
- norm_gain: float32 [2, 768], P(None, 'dp'), may hold values from 0.5 to 1.5
- gate_weight: float32 [2, 768, 1536], P(None, 'dp'), may hold values from -0.21875 to 0.21875
- mix_weight: float32 [2, 768, 1792], P(None, 'dp'), may hold values from -0.21875 to 0.21875
- step_weight: float32 [2, 768, 24], P(None, 'dp'), may hold values from -0.21875 to 0.21875
- conv_kernel: float32 [2, 4, 1792], P(None, None, 'dp'), may hold values from -0.5 to 0.5
- conv_bias: float32 [2, 1792], P(None, 'dp'), may hold values from -0.5 to 0.5
- gated_gain: float32 [2, 1536], P(None, 'dp'), may hold values from 0.5 to 1.5
- out_weight: float32 [2, 1536, 768], P(None, 'dp'), may hold values from -0.15625 to 0.15625
- skip_gain: float32 [2, 24], replicated, may hold values from 0.5 to 1.5
- log_rate: float32 [2, 24], replicated, may hold values from -4 to 1
- step_bias: float32 [2, 24], replicated, may hold values from -9 to -4
Outputs:
- result: float32 [4, 2048, 768], P('dp', 'seq')
- hidden_grad: float32 [4, 2048, 768], P('dp', 'seq')
- norm_gain_grad: float32 [2, 768], P(None, 'dp')
- gate_weight_grad: float32 [2, 768, 1536], P(None, 'dp')
- mix_weight_grad: float32 [2, 768, 1792], P(None, 'dp')
- step_weight_grad: float32 [2, 768, 24], P(None, 'dp')
- conv_kernel_grad: float32 [2, 4, 1792], P(None, None, 'dp')
- conv_bias_grad: float32 [2, 1792], P(None, 'dp')
- gated_gain_grad: float32 [2, 1536], P(None, 'dp')
- out_weight_grad: float32 [2, 1536, 768], P(None, 'dp')
- skip_gain_grad: float32 [2, 24], replicated
Inputs may be any that keep to these rules, and one draw needn't show every extreme that they name: `lengths`: positions at or past a slot's length are padding; some slot has length 2048 and some slot the least length.
All inputs are finite; a program needn't handle non-finite values.
Results may differ from a plain program's by a relative error of at most 0.0003.
Values sent between devices are 32-bit elements; how exact they have to be, the bound alone decides.
A program may use at most 192 MiB of HBM per device.

v0:
```python
import jax
import jax.numpy as jnp
from jax import lax
from jax.sharding import PartitionSpec as P

EPSILON = 1e-05
HIGHEST = lax.Precision.HIGHEST


def from_behind(value, axis, steps):
    count = lax.axis_size(axis)
    first, last = (max(0, -steps), min(count, count - steps))
    return lax.ppermute(value, axis, [(source, source + steps) for source in range(first, last)])


def matmul(left, right):
    return jnp.dot(left, right, precision=HIGHEST)


def rms_scale(values):
    return lax.rsqrt(jnp.mean(values * values, axis=-1, keepdims=True) + EPSILON)


def carry_forward(totals, state_local):

    def relay_turn(turn_index, incoming):
        return from_behind(totals[:, :, None, None] * incoming + state_local, "seq", 1)

    return lax.fori_loop(0, lax.axis_size("seq") - 1, relay_turn, jnp.zeros_like(state_local))


def carry_backward(totals, state_in_grad):

    def relay_back(turn_index, incoming):
        return from_behind(totals[:, :, None, None] * incoming + state_in_grad, "seq", -1)

    return lax.fori_loop(0, lax.axis_size("seq") - 1, relay_back, jnp.zeros_like(state_in_grad))


def layer_forward(stream, weights, skip_gain, log_rate, step_bias):
    (
        norm_gain,
        gate_weight,
        mix_weight,
        step_weight,
        conv_kernel,
        conv_bias,
        gated_gain,
        out_weight,
    ) = weights
    slots, group, width = stream.shape
    inner = gated_gain.shape[0]
    heads = skip_gain.shape[0]
    head_size = inner // heads
    taps = conv_kernel.shape[0]
    flat = stream.reshape(slots * group, width)
    inv_in = rms_scale(flat)
    normed = flat * inv_in * norm_gain
    gate_pre = matmul(normed, gate_weight)
    mixed_raw = matmul(normed, mix_weight).reshape(slots, group, -1)
    step_raw = matmul(normed, step_weight).reshape(slots, group, heads)
    channels = mixed_raw.shape[-1]
    states = (channels - inner) // 2
    edge = from_behind(mixed_raw[:, group - taps + 1 :, :], "seq", 1)
    extended = jnp.concatenate([edge, mixed_raw], axis=1)
    conv_pre = conv_bias
    for tap_index in range(taps):
        conv_pre = conv_pre + conv_kernel[tap_index] * extended[:, tap_index : tap_index + group, :]
    mixed = jax.nn.silu(conv_pre)
    heads_in = mixed[..., :inner].reshape(slots, group, heads, head_size)
    input_map = mixed[..., inner : inner + states]
    output_map = mixed[..., inner + states :]
    step_size = jax.nn.softplus(step_raw + step_bias)
    rates = jnp.exp(log_rate)
    log_decay = jnp.cumsum(-rates * step_size, axis=1)
    scaled_in = heads_in * step_size[..., None]
    position = lax.iota(jnp.int32, group)
    causal = (position[:, None] >= position[None, :])[None, :, :, None]
    gaps = log_decay[:, :, None, :] - log_decay[:, None, :, :]
    decays = jnp.where(causal, jnp.exp(jnp.where(causal, gaps, 0.0)), 0.0)
    intersection = jnp.einsum("btn,bsn->bts", output_map, input_map, precision=HIGHEST)
    mixing = intersection[..., None] * decays
    diag_out = jnp.einsum("btsh,bshp->bthp", mixing, scaled_in, precision=HIGHEST)
    end_weight = jnp.exp(log_decay[:, -1:, :] - log_decay)
    state_local = jnp.einsum(
        "bshp,bsn->bhpn", scaled_in * end_weight[..., None], input_map, precision=HIGHEST
    )
    totals = jnp.exp(log_decay[:, -1, :])
    state_in = carry_forward(totals, state_local)
    lift = jnp.exp(log_decay)
    off_out = lift[..., None] * jnp.einsum(
        "btn,bhpn->bthp", output_map, state_in, precision=HIGHEST
    )
    mixed_out = diag_out + off_out + skip_gain[:, None] * heads_in
    out_flat = mixed_out.reshape(slots * group, inner)
    gate_sig = jax.nn.sigmoid(gate_pre)
    gated = out_flat * (gate_pre * gate_sig)
    inv_out = rms_scale(gated)
    normed_out = gated * inv_out * gated_gain
    branch = matmul(normed_out, out_weight)
    saved = {
        "flat": flat,
        "inv_in": inv_in,
        "normed": normed,
        "gate_pre": gate_pre,
        "gate_sig": gate_sig,
        "step_raw": step_raw,
        "extended": extended,
        "conv_pre": conv_pre,
        "heads_in": heads_in,
        "input_map": input_map,
        "output_map": output_map,
        "step_size": step_size,
        "scaled_in": scaled_in,
        "decays": decays,
        "mixing": mixing,
        "end_weight": end_weight,
        "totals": totals,
        "state_in": state_in,
        "lift": lift,
        "off_out": off_out,
        "out_flat": out_flat,
        "gated": gated,
        "inv_out": inv_out,
        "normed_out": normed_out,
    }
    return (stream + branch.reshape(slots, group, width), saved)


def layer_backward(grad, saved, weights, skip_gain, log_rate, step_bias):
    (
        norm_gain,
        gate_weight,
        mix_weight,
        step_weight,
        conv_kernel,
        conv_bias,
        gated_gain,
        out_weight,
    ) = weights
    slots, group, width = grad.shape
    inner = gated_gain.shape[0]
    heads = skip_gain.shape[0]
    head_size = inner // heads
    taps = conv_kernel.shape[0]
    flat = saved["flat"]
    inv_in = saved["inv_in"]
    normed = saved["normed"]
    gate_pre = saved["gate_pre"]
    gate_sig = saved["gate_sig"]
    heads_in = saved["heads_in"]
    input_map = saved["input_map"]
    output_map = saved["output_map"]
    scaled_in = saved["scaled_in"]
    end_weight = saved["end_weight"]
    totals = saved["totals"]
    state_in = saved["state_in"]
    mixing = saved["mixing"]
    gated = saved["gated"]
    inv_out = saved["inv_out"]
    conv_pre = saved["conv_pre"]
    extended = saved["extended"]
    channels = extended.shape[-1]
    grad_flat = grad.reshape(slots * group, width)
    out_weight_grad = matmul(saved["normed_out"].T, grad_flat)
    normed_out_grad = matmul(grad_flat, out_weight.T)
    gated_gain_grad = jnp.sum(normed_out_grad * gated * inv_out, axis=0)
    scaled = normed_out_grad * gated_gain
    gated_grad = inv_out * scaled - gated * (inv_out * inv_out * inv_out) * jnp.mean(
        scaled * gated, axis=-1, keepdims=True
    )
    gate_grad = gated_grad * saved["out_flat"] * gate_sig * (1.0 + gate_pre * (1.0 - gate_sig))
    out_grad = (gated_grad * (gate_pre * gate_sig)).reshape(slots, group, heads, head_size)
    skip_grad = jnp.sum(out_grad * heads_in, axis=(0, 1, 3))
    heads_grad = skip_gain[:, None] * out_grad
    lifted_grad = out_grad * saved["lift"][..., None]
    state_in_grad = jnp.einsum("bthp,btn->bhpn", lifted_grad, output_map, precision=HIGHEST)
    output_map_grad = jnp.einsum("bthp,bhpn->btn", lifted_grad, state_in, precision=HIGHEST)
    decay_grad = jnp.sum(out_grad * saved["off_out"], axis=-1)
    pairing = jnp.einsum("bthp,bshp->btsh", out_grad, scaled_in, precision=HIGHEST)
    scaled_grad = jnp.einsum("btsh,bthp->bshp", mixing, out_grad, precision=HIGHEST)
    intersection_grad = jnp.sum(saved["decays"] * pairing, axis=-1)
    output_map_grad = output_map_grad + jnp.einsum(
        "bts,bsn->btn", intersection_grad, input_map, precision=HIGHEST
    )
    input_map_grad = jnp.einsum("bts,btn->bsn", intersection_grad, output_map, precision=HIGHEST)
    weighted = mixing * pairing
    decay_grad = decay_grad + jnp.sum(weighted, axis=2) - jnp.sum(weighted, axis=1)
    state_out_grad = carry_backward(totals, state_in_grad)
    end_grad = jnp.sum(state_out_grad * state_in, axis=(2, 3)) * totals
    reach = jnp.einsum("bhpn,bsn->bshp", state_out_grad, input_map, precision=HIGHEST)
    scaled_grad = scaled_grad + reach * end_weight[..., None]
    input_map_grad = input_map_grad + jnp.einsum(
        "bshp,bhpn->bsn", scaled_in * end_weight[..., None], state_out_grad, precision=HIGHEST
    )
    weight_pull = jnp.sum(reach * scaled_in, axis=-1) * end_weight
    end_grad = end_grad + jnp.sum(weight_pull, axis=1)
    decay_grad = decay_grad - weight_pull
    decay_grad = jnp.concatenate(
        [decay_grad[:, :-1, :], decay_grad[:, -1:, :] + end_grad[:, None, :]], axis=1
    )
    rate_grad = jnp.flip(jnp.cumsum(jnp.flip(decay_grad, axis=1), axis=1), axis=1)
    step_grad = -jnp.exp(log_rate) * rate_grad + jnp.sum(scaled_grad * heads_in, axis=-1)
    heads_grad = heads_grad + scaled_grad * saved["step_size"][..., None]
    step_raw_grad = step_grad * jax.nn.sigmoid(saved["step_raw"] + step_bias)
    mixed_grad = jnp.concatenate(
        [heads_grad.reshape(slots, group, inner), input_map_grad, output_map_grad], axis=-1
    )
    conv_sig = jax.nn.sigmoid(conv_pre)
    pre_grad = mixed_grad * conv_sig * (1.0 + conv_pre * (1.0 - conv_sig))
    conv_bias_grad = jnp.sum(pre_grad, axis=(0, 1))
    conv_kernel_grad = jnp.stack(
        [
            jnp.sum(pre_grad * extended[:, tap_index : tap_index + group, :], axis=(0, 1))
            for tap_index in range(taps)
        ]
    )
    border = jnp.zeros((slots, taps - 1, channels), jnp.float32)
    padded_grad = jnp.concatenate([border, pre_grad, border], axis=1)
    extended_grad = conv_kernel[0] * padded_grad[:, taps - 1 : taps - 1 + group + taps - 1, :]
    for tap_index in range(1, taps):
        offset = taps - 1 - tap_index
        extended_grad = (
            extended_grad
            + conv_kernel[tap_index] * padded_grad[:, offset : offset + group + taps - 1, :]
        )
    edge_back = from_behind(extended_grad[:, : taps - 1, :], "seq", -1)
    raw_grad = extended_grad[:, taps - 1 :, :]
    raw_grad = jnp.concatenate(
        [raw_grad[:, : group - taps + 1, :], raw_grad[:, group - taps + 1 :, :] + edge_back], axis=1
    )
    raw_flat = raw_grad.reshape(slots * group, channels)
    step_flat = step_raw_grad.reshape(slots * group, heads)
    gate_weight_grad = matmul(normed.T, gate_grad)
    mix_weight_grad = matmul(normed.T, raw_flat)
    step_weight_grad = matmul(normed.T, step_flat)
    normed_grad = (
        matmul(gate_grad, gate_weight.T)
        + matmul(raw_flat, mix_weight.T)
        + matmul(step_flat, step_weight.T)
    )
    norm_gain_grad = jnp.sum(normed_grad * flat * inv_in, axis=0)
    scaled_norm = normed_grad * norm_gain
    stream_grad = (
        grad_flat
        + inv_in * scaled_norm
        - flat * (inv_in * inv_in * inv_in) * jnp.mean(scaled_norm * flat, axis=-1, keepdims=True)
    )
    weight_grads = (
        norm_gain_grad,
        gate_weight_grad,
        mix_weight_grad,
        step_weight_grad,
        conv_kernel_grad,
        conv_bias_grad,
        gated_gain_grad,
        out_weight_grad,
    )
    return (stream_grad.reshape(slots, group, width), weight_grads, skip_grad)


def on_device(
    hidden,
    cotangent,
    lengths,
    norm_gain,
    gate_weight,
    mix_weight,
    step_weight,
    conv_kernel,
    conv_bias,
    gated_gain,
    out_weight,
    skip_gain,
    log_rate,
    step_bias,
):
    slots, group, width = hidden.shape
    layers = norm_gain.shape[0]
    position = lax.axis_index("seq") * group + lax.iota(jnp.int32, group)
    mask = (position[None, :] < lengths[:, None]).astype(jnp.float32)[:, :, None]
    stream = hidden
    saved_all = []
    for layer_index in range(layers):
        weights = (
            lax.all_gather(norm_gain[layer_index], "dp", axis=0, tiled=True),
            lax.all_gather(gate_weight[layer_index], "dp", axis=0, tiled=True),
            lax.all_gather(mix_weight[layer_index], "dp", axis=0, tiled=True),
            lax.all_gather(step_weight[layer_index], "dp", axis=0, tiled=True),
            lax.all_gather(conv_kernel[layer_index], "dp", axis=1, tiled=True),
            lax.all_gather(conv_bias[layer_index], "dp", axis=0, tiled=True),
            lax.all_gather(gated_gain[layer_index], "dp", axis=0, tiled=True),
            lax.all_gather(out_weight[layer_index], "dp", axis=0, tiled=True),
        )
        stream, saved = layer_forward(
            stream, weights, skip_gain[layer_index], log_rate[layer_index], step_bias[layer_index]
        )
        saved_all.append(saved)
    result = stream * mask
    grad = cotangent * mask
    reduced_all = []
    skip_all = []
    for layer_index in reversed(range(layers)):
        weights = (
            lax.all_gather(norm_gain[layer_index], "dp", axis=0, tiled=True),
            lax.all_gather(gate_weight[layer_index], "dp", axis=0, tiled=True),
            lax.all_gather(mix_weight[layer_index], "dp", axis=0, tiled=True),
            lax.all_gather(step_weight[layer_index], "dp", axis=0, tiled=True),
            lax.all_gather(conv_kernel[layer_index], "dp", axis=1, tiled=True),
            lax.all_gather(conv_bias[layer_index], "dp", axis=0, tiled=True),
            lax.all_gather(gated_gain[layer_index], "dp", axis=0, tiled=True),
            lax.all_gather(out_weight[layer_index], "dp", axis=0, tiled=True),
        )
        grad, weight_grads, skip_grad = layer_backward(
            grad,
            saved_all[layer_index],
            weights,
            skip_gain[layer_index],
            log_rate[layer_index],
            step_bias[layer_index],
        )
        reduced = (
            lax.psum_scatter(weight_grads[0], "dp", scatter_dimension=0, tiled=True),
            lax.psum_scatter(weight_grads[1], "dp", scatter_dimension=0, tiled=True),
            lax.psum_scatter(weight_grads[2], "dp", scatter_dimension=0, tiled=True),
            lax.psum_scatter(weight_grads[3], "dp", scatter_dimension=0, tiled=True),
            lax.psum_scatter(weight_grads[4], "dp", scatter_dimension=1, tiled=True),
            lax.psum_scatter(weight_grads[5], "dp", scatter_dimension=0, tiled=True),
            lax.psum_scatter(weight_grads[6], "dp", scatter_dimension=0, tiled=True),
            lax.psum_scatter(weight_grads[7], "dp", scatter_dimension=0, tiled=True),
        )
        reduced = lax.psum(
            (
                reduced[0],
                reduced[1],
                reduced[2],
                reduced[3],
                reduced[4],
                reduced[5],
                reduced[6],
                reduced[7],
            ),
            "seq",
        )
        skip_total = lax.psum(skip_grad, ("dp", "seq"))
        reduced_all.insert(0, reduced)
        skip_all.insert(0, skip_total)
    stacked = tuple((jnp.stack([entry[member] for entry in reduced_all]) for member in range(8)))
    return (result, grad) + stacked + (jnp.stack(skip_all),)


def solution(mesh):
    return jax.shard_map(
        on_device,
        mesh=mesh,
        in_specs=(
            P("dp", "seq", None),
            P("dp", "seq", None),
            P("dp"),
            P(None, "dp"),
            P(None, "dp", None),
            P(None, "dp", None),
            P(None, "dp", None),
            P(None, None, "dp"),
            P(None, "dp"),
            P(None, "dp"),
            P(None, "dp", None),
            P(),
            P(),
            P(),
        ),
        out_specs=(
            P("dp", "seq", None),
            P("dp", "seq", None),
            P(None, "dp"),
            P(None, "dp", None),
            P(None, "dp", None),
            P(None, "dp", None),
            P(None, None, "dp"),
            P(None, "dp"),
            P(None, "dp"),
            P(None, "dp", None),
            P(),
        ),
        check_vma=False,
    )
```

profile of v0, /device:TPU:0, one launch (start us, length us, event | category | flops | bytes accessed | tf_op | source)
XLA Modules:
  0.0 1350.7 jit_solution(13960874902507613550)
XLA Ops:
  17.8 14.1 %all-gather.4 = f32[1,768,24]{2,0,1:T(1,128)S(1)} all-gather(f32[1,192,24]{2,0,1:T(1,128)S(1)} %copy.514), channel_id=6, replica_groups=mesh['dp'=4,'seq'=8] {'dp'}, dimensions={1}, use_global_device_ids=true | all-gather | bytes 92160 | tf_op jit(solution)/shard_map/all_gather | solution.py:289
  36.6 16.4 %all-reduce.18 = (f32[768]{0:T(1024)S(1)}, f32[1792]{0:T(1024)}, f32[768]{0:T(1024)S(1)}, f32[1792]{0:T(1024)}) all-reduce(f32[768]{0:T(1024)S(1)} %dynamic-update-slice.1, f32[1792]{0:T(1024)S(1)} %dynamic-update-slice, f32[768]{0:T(1024)S(1)} %dynamic-update-slice.3, ...), channel_id=4, replica_groups=mesh['dp'=4,'seq'=8] {'dp'}, use_global_device_ids=true, to_apply=%add.5 | all-reduce | flops 5120 | bytes 40960 | tf_op jit(solution)/shard_map/all_gather | solution.py:286
  56.2 20.5 %all-gather.1 = f32[1,4,1792]{1,0,2:T(1,128)S(1)} all-gather(f32[1,4,448]{1,0,2:T(1,128)S(1)} %copy.513), channel_id=3, replica_groups=mesh['dp'=4,'seq'=8] {'dp'}, dimensions={2}, use_global_device_ids=true | all-gather | bytes 35840 | tf_op jit(solution)/shard_map/all_gather | solution.py:290
  76.8 37.7 %slice_reduce_fusion.7 = (f32[1792]{0:T(1024)}, f32[1792]{0:T(1024)}, f32[1792]{0:T(1024)}, f32[1792]{0:T(1024)}) fusion(f32[1,4,1792]{1,0,2:T(1,128)S(1)} %all-gather.1), kind=kLoop, calls=%fused_computation.195 | loop fusion | bytes 57344 | tf_op jit(solution)/shard_map/slice | solution.py:68
  115.3 17.0 %all-gather.9 = f32[1,4,1792]{1,0,2:T(1,128)S(1)} all-gather(f32[1,4,448]{1,0,2:T(1,128)S(1)} %copy.515), channel_id=11, replica_groups=mesh['dp'=4,'seq'=8] {'dp'}, dimensions={2}, use_global_device_ids=true | all-gather | bytes 35840 | tf_op jit(solution)/shard_map/all_gather | solution.py:290
  132.3 37.9 %slice_reduce_fusion.3 = (f32[1792]{0:T(1024)}, f32[1792]{0:T(1024)}, f32[1792]{0:T(1024)}, f32[1792]{0:T(1024)}) fusion(f32[1,4,1792]{1,0,2:T(1,128)S(1)} %all-gather.9), kind=kLoop, calls=%fused_computation.191 | loop fusion | bytes 57344 | tf_op jit(solution)/shard_map/slice | solution.py:68
  229.8 90.3 %while.40 = (s32[]{:T(128)}, f32[1,24,64,128]{3,2,1,0:T(8,128)S(1)}, f32[1,24]{1,0:T(1,128)}, f32[1,24,64,128]{3,2,1,0:T(8,128)S(1)}, s32[]{:T(128)}) while((s32[]{:T(128)}, f32[1,24,64,128]{3,2,1,0:T(8,128)S(1)}, f32[1,24]{1,0:T(1,128)}, f32[1,24,64,128]{3,2,1,0:T(8,128)S(1)}, s32[]{:T(128)}) %tuple.134), condition=%wide.region_4.5_spmd, body=%wide.region_3.4_spmd.sunk | while | flops 393218 | bytes 5505221 | solution.py:29
  405.7 100.9 %while.41 = (s32[]{:T(128)}, f32[1,24,64,128]{3,2,1,0:T(8,128)S(1)}, f32[1,24]{1,0:T(1,128)}, f32[1,24,64,128]{3,2,1,0:T(8,128)}, s32[]{:T(128)}) while((s32[]{:T(128)}, f32[1,24,64,128]{3,2,1,0:T(8,128)S(1)}, f32[1,24]{1,0:T(1,128)}, f32[1,24,64,128]{3,2,1,0:T(8,128)}, s32[]{:T(128)}) %tuple.137), condition=%wide.region_10.11_spmd, body=%wide.region_9.10_spmd.sunk | while | flops 393218 | bytes 5505221 | solution.py:29
  571.8 114.4 %while.42 = (s32[]{:T(128)}, f32[1,24,64,128]{3,2,1,0:T(8,128)}, f32[1,24]{1,0:T(1,128)}, f32[1,24,64,128]{3,2,1,0:T(8,128)}, s32[]{:T(128)}) while((s32[]{:T(128)}, f32[1,24,64,128]{3,2,1,0:T(8,128)}, f32[1,24]{1,0:T(1,128)}, f32[1,24,64,128]{3,2,1,0:T(8,128)}, s32[]{:T(128)}) %tuple.182), condition=%wide.region_14.15_spmd, body=%wide.region_13.14_spmd.sunk | while | flops 393218 | bytes 5505221 | solution.py:37
  591.7 13.3 collective-permute-done.2
  608.6 12.6 collective-permute-done.2
  624.9 12.6 collective-permute-done.2
  641.2 12.7 collective-permute-done.2
  657.7 12.5 collective-permute-done.2
  823.5 111.6 %while.43 = (s32[]{:T(128)}, f32[1,24,64,128]{3,2,1,0:T(8,128)S(1)}, f32[1,24]{1,0:T(1,128)S(1)}, f32[1,24,64,128]{3,2,1,0:T(8,128)}, s32[]{:T(128)}) while((s32[]{:T(128)}, f32[1,24,64,128]{3,2,1,0:T(8,128)S(1)}, f32[1,24]{1,0:T(1,128)S(1)}, f32[1,24,64,128]{3,2,1,0:T(8,128)}, s32[]{:T(128)}) %tuple.181), condition=%wide.region_28.29_spmd, body=%wide.region_27.28_spmd.sunk | while | flops 393218 | bytes 5505221 | solution.py:37
  843.1 12.7 collective-permute-done.3
  874.9 12.6 collective-permute-done.3
  922.5 12.6 collective-permute-done.3
  1005.1 51.9 %reduce-scatter.23.cloned.1.call-done = f32[192,1792]{1,0:T(8,128)} async-done(((f32[768,1792]{1,0:T(8,128)}), f32[192,1792]{1,0:T(8,128)}) %reduce-scatter.23.cloned.1.call-update) | async-done | bytes 1376272 | tf_op jit(solution)/shard_map/reduce_scatter | solution.py:325
  1066.8 39.6 %all-reduce.14 = (f32[1,24]{1,0:T(1,128)S(1)}, f32[1,24]{1,0:T(1,128)S(1)}) all-reduce(f32[1,24]{1,0:T(1,128)S(1)} %bitcast.663, f32[1,24]{1,0:T(1,128)S(1)} %bitcast.664), channel_id=1, replica_groups=mesh['dp'=4,'seq'=8] {'dp','seq'}, use_global_device_ids=true, to_apply=%region_91.92 | all-reduce | flops 48 | bytes 384 | tf_op jit(solution)/shard_map/psum | solution.py:345
  1122.7 17.5 %all-reduce.17 = (f32[768]{0:T(1024)S(1)}, f32[768]{0:T(1024)S(1)}, f32[1792]{0:T(1024)S(1)}, f32[1792]{0:T(1024)S(1)}, f32[1536]{0:T(1024)S(1)}, /*index=5*/f32[1536]{0:T(1024)S(1)}) all-reduce(f32[768]{0:T(1024)S(1)} %copy-done.142, f32[768]{0:T(1024)S(1)} %get-tuple-element.129, ...), channel_id=19, replica_groups=mesh['dp'=4,'seq'=8] {'dp'}, use_global_device_ids=true, to_apply=%region_44.45.clone | all-reduce | flops 8192 | bytes 65536
  1146.3 26.1 %reduce-scatter.31.cloned.1.call-done = f32[192,24]{1,0:T(8,128)} async-done(((f32[768,24]{1,0:T(8,128)}), f32[192,24]{1,0:T(8,128)}) %reduce-scatter.31.cloned.1.call-update) | async-done | bytes 18448
  1173.3 31.6 %all-reduce.15 = (f32[1,192]{1,0:T(1,128)S(1)}, f32[1,192]{1,0:T(1,128)S(1)}, f32[1,192,24]{1,2,0:T(8,128)S(1)}, f32[1,192,24]{1,2,0:T(8,128)S(1)}, f32[1,4,448]...) all-reduce(f32[1,192]{1,0:T(1,128)S(1)} %bitcast.655, ...), channel_id=1, replica_groups=mesh['dp'=4,'seq'=8] {'seq'}, use_global_device_ids=true, to_apply=%region_45.46 | all-reduce | flops 14848 | bytes 118784 | tf_op jit(solution)/shard_map/psum | solution.py:332
  1207.9 128.5 %all-reduce.21.cloned.1.call-done = (f32[1,192,1536]{2,1,0:T(8,128)}, f32[1,192,1536]{2,1,0:T(8,128)}, f32[1,192,1792]{2,1,0:T(8,128)}, f32[1,192,1792]{2,1,0:T(...) async-done(((f32[1,192,1536]{2,1,0:T(8,128)}, f32[1,192,1536]{2,1,0:T(8,128)}, f32[1,192,1792]{2,1,0:T(8,128)}, f32[1,192,1792]{2,1,0:T(8,128)}, ...) | async-done | bytes 7471120 | tf_op jit(solution)/shard_map/psum | solution.py:332
  (728 shorter events, 788.2 us)
Async XLA Ops:
  7.2 163.7 %all-gather.23.cloned.1.call-start = ((), (), s32[]{:S(2)}) async-start(), calls=%async_computation.16 | async-start | bytes 6881280 | tf_op jit(solution)/shard_map/all_gather | solution.py:288
  10.9 323.2 %all-gather.25.cloned.1.call-start = ((), (), s32[]{:S(2)}) async-start(), calls=%async_computation.17 | async-start | bytes 5898240 | tf_op jit(solution)/shard_map/all_gather | solution.py:287
  12.5 331.4 %all-gather.27.cloned.1.call-start = ((), (), s32[]{:S(2)}) async-start(), calls=%async_computation.18 | async-start | bytes 5898240 | tf_op jit(solution)/shard_map/all_gather | solution.py:293
  15.8 338.2 %all-gather.29.cloned.1.call-start = ((), (), s32[]{:S(2)}) async-start(), calls=%async_computation.19 | async-start | bytes 6881280 | tf_op jit(solution)/shard_map/all_gather | solution.py:288
  16.4 504.2 %all-gather.31.cloned.1.call-start = ((), (), s32[]{:S(2)}) async-start(), calls=%async_computation.20 | async-start | bytes 5898240 | tf_op jit(solution)/shard_map/all_gather | solution.py:287
  17.0 513.9 %all-gather.33.cloned.1.call-start = ((), (), s32[]{:S(2)}) async-start(), calls=%async_computation.21 | async-start | bytes 5898240 | tf_op jit(solution)/shard_map/all_gather | solution.py:293
  17.6 987.4 %reduce-scatter.21.cloned.1.call-start = ((), (), s32[]{:S(2)}) async-start(), calls=%async_computation.11 | async-start | bytes 5898240 | tf_op jit(solution)/shard_map/reduce_scatter | solution.py:324
  179.0 37.5 %collective-permute-start.4 = (f32[1,3,1792]{2,1,0:T(4,128)}, f32[1,3,1792]{2,1,0:T(4,128)S(1)}, u32[]{:S(2)}, u32[]{:S(2)}) collective-permute-start(f32[1,3,1792]{2,1,0:T(4,128)} %slice.331), channel_id=1, source_target_pairs={{0,1},{1,2},{2,3},{3,4},{4,5},{5,6},{6,7},{8,9},{9,10},{10,11},{11... | collective-permute-start | bytes 64520 | tf_op jit(solution)/shard_map/ppermute | solution.py:13
  235.1 14.3 %collective-permute-start = (f32[1,24,64,128]{3,2,1,0:T(8,128)S(1)}, f32[1,24,64,128]{3,2,1,0:T(8,128)S(1)}, u32[]{:S(2)}, u32[]{:S(2)}) collective-permute-start(f32[1,24,64,128]{3,2,1,0:T(8,128)S(1)} %multiply_add_fusion.10), channel_id=1, source_target_pairs={{0,1},{1,2},{2,3},{3,4},{4,5},{5,6},{6,7},{8,9},{9,10},{10,11},{11... | collective-permute-start | bytes 2359304 | tf_op jit(solution)/shard_map/while/body/eval_jaxpr/ppermute | solution.py:13
  362.6 23.0 %collective-permute-start.5 = (f32[1,3,1792]{2,1,0:T(4,128)S(1)}, f32[1,3,1792]{2,1,0:T(4,128)S(1)}, u32[]{:S(2)}, u32[]{:S(2)}) collective-permute-start(f32[1,3,1792]{2,1,0:T(4,128)S(1)} %slice.345), channel_id=1, source_target_pairs={{0,1},{1,2},{2,3},{3,4},{4,5},{5,6},{6,7},{8,9},{9,10},{10,11},{11... | collective-permute-start | bytes 64520 | tf_op jit(solution)/shard_map/ppermute | solution.py:13
  549.3 455.7 %reduce-scatter.29.cloned.1.call-start = ((), (), s32[]{:S(2)}) async-start(), calls=%async_computation.15 | async-start | bytes 5898240 | tf_op jit(solution)/shard_map/reduce_scatter | solution.py:330
  570.8 434.3 %reduce-scatter.19.cloned.1.call-start = ((), (), s32[]{:S(2)}) async-start(), calls=%async_computation.10 | async-start | bytes 5898240 | tf_op jit(solution)/shard_map/reduce_scatter | solution.py:324
  590.4 14.6 %collective-permute-start.2 = (f32[1,24,64,128]{3,2,1,0:T(8,128)}, f32[1,24,64,128]{3,2,1,0:T(8,128)}, u32[]{:S(2)}, u32[]{:S(2)}) collective-permute-start(f32[1,24,64,128]{3,2,1,0:T(8,128)} %multiply_add_fusion.12), channel_id=1, source_target_pairs={{1,0},{2,1},{3,2},{4,3},{5,4},{6,5},{7,6},{9,8},{10,9},{11,10},{12... | collective-permute-start | bytes 2359304 | tf_op jit(solution)/shard_map/while/body/eval_jaxpr/ppermute | solution.py:13
  639.9 14.0 %collective-permute-start.2 = (f32[1,24,64,128]{3,2,1,0:T(8,128)}, f32[1,24,64,128]{3,2,1,0:T(8,128)}, u32[]{:S(2)}, u32[]{:S(2)}) collective-permute-start(f32[1,24,64,128]{3,2,1,0:T(8,128)} %multiply_add_fusion.12), channel_id=1, source_target_pairs={{1,0},{2,1},{3,2},{4,3},{5,4},{6,5},{7,6},{9,8},{10,9},{11,10},{12... | collective-permute-start | bytes 2359304 | tf_op jit(solution)/shard_map/while/body/eval_jaxpr/ppermute | solution.py:13
  737.2 23.4 %collective-permute-start.6 = (f32[1,3,1792]{2,1,0:T(4,128)}, f32[1,3,1792]{2,1,0:T(4,128)}, u32[]{:S(2)}, u32[]{:S(2)}) collective-permute-start(f32[1,3,1792]{2,1,0:T(4,128)} %slice.362), channel_id=1, source_target_pairs={{1,0},{2,1},{3,2},{4,3},{5,4},{6,5},{7,6},{9,8},{10,9},{11,10},{12... | collective-permute-start | bytes 64520 | tf_op jit(solution)/shard_map/ppermute | solution.py:13
  787.3 217.7 %reduce-scatter.27.cloned.1.call-start = ((), (), s32[]{:S(2)}) async-start(), calls=%async_computation.14 | async-start | bytes 5898240 | tf_op jit(solution)/shard_map/reduce_scatter | solution.py:330
  795.0 210.1 %reduce-scatter.25.cloned.1.call-start = ((), (), s32[]{:S(2)}) async-start(), calls=%async_computation.13 | async-start | bytes 6881280 | tf_op jit(solution)/shard_map/reduce_scatter | solution.py:325
  803.7 253.3 %reduce-scatter.23.cloned.1.call-start = ((), (), s32[]{:S(2)}) async-start(), calls=%async_computation.12 | async-start | bytes 6881280 | tf_op jit(solution)/shard_map/reduce_scatter | solution.py:325
  841.8 14.0 %collective-permute-start.3 = (f32[1,24,64,128]{3,2,1,0:T(8,128)}, f32[1,24,64,128]{3,2,1,0:T(8,128)S(1)}, u32[]{:S(2)}, u32[]{:S(2)}) collective-permute-start(f32[1,24,64,128]{3,2,1,0:T(8,128)} %multiply_add_fusion.13), channel_id=1, source_target_pairs={{1,0},{2,1},{3,2},{4,3},{5,4},{6,5},{7,6},{9,8},{10,9},{11,10},{12... | collective-permute-start | bytes 2359304 | tf_op jit(solution)/shard_map/while/body/eval_jaxpr/ppermute | solution.py:13
  991.9 149.9 %reduce-scatter.37.cloned.1.call-start = ((), (), s32[]{:S(2)}) async-start(), calls=%async_computation.25 | async-start | bytes 1146880
  994.0 148.9 %reduce-scatter.35.cloned.1.call-start = ((), (), s32[]{:S(2)}) async-start(), calls=%async_computation.24 | async-start | bytes 1146880
  995.4 149.9 %reduce-scatter.33.cloned.1.call-start = ((), (), s32[]{:S(2)}) async-start(), calls=%async_computation.23 | async-start | bytes 491520
  997.7 174.7 %reduce-scatter.31.cloned.1.call-start = ((), (), s32[]{:S(2)}) async-start(), calls=%async_computation.22 | async-start | bytes 491520
  1004.9 331.5 %all-reduce.21.cloned.1.call-start = ((), (), s32[]{:S(2)}) async-start(), calls=%async_computation.26 | async-start | bytes 14942208 | tf_op jit(solution)/shard_map/psum | solution.py:332
  (195 other events, 2256.9 us)
Sparse Core Ops, SparseCore 0:
  11.0 76.4 all-gather.22
  89.3 60.2 all-gather.24
  151.5 57.4 all-gather.26
  210.7 65.1 all-gather.28
  277.6 57.0 all-gather.30
  336.4 57.0 all-gather.32
  549.4 66.9 reduce-scatter.20
  619.4 57.0 reduce-scatter.28
  787.5 66.5 reduce-scatter.18
  856.9 57.0 reduce-scatter.26
  917.1 63.6 reduce-scatter.24
  992.0 64.8 reduce-scatter.22
  1060.5 27.1 reduce-scatter.36
  1091.0 27.0 reduce-scatter.34
  1120.7 24.5 reduce-scatter.32
  1148.0 24.3 reduce-scatter.30
  1175.1 161.2 all-reduce.20
where the time goes:
time: 1360 us; the launch traced here: 1350 us
  waiting for transfers between devices  424 us (31%)
  matrix products  246 us (18%)
  local copies, waits for them, and re-layouts  189 us (14%)
  blocking collectives  181 us (13%)
  starting transfers between devices  176 us (13%)
  other arithmetic  112 us (8%)
  between operations  20.5 us (2%)
    ppermute x32, waiting for transfers between devices, from_behind(): lax.ppermute(value, axis, [(source, source + steps) for source in range(f...  214 us
    ppermute x32, starting transfers between devices, from_behind(): lax.ppermute(value, axis, [(source, source + steps) for source in range(f...  175 us
    dot_general x22, matrix products, matmul(): return jnp.dot(left, right, precision=HIGHEST)  136 us
    psum x1, waiting for transfers between devices, on_device(): lax.psum((reduced[0], reduced[1], reduced[2], reduced[3], reduced[4], red...  128 us
    slice x2, local copies, waits for them, and re-layouts, layer_forward(): conv_kernel[tap_index] * extended[:, tap_index:tap_index + group, :]  75.7 us
    reduce_scatter x2, waiting for transfers between devices, on_device(): lax.psum_scatter(weight_grads[2], 'dp', scatter_dimension=0, tiled=True)  51.9 us
    psum x1, blocking collectives, on_device(): skip_total = lax.psum(skip_grad, ('dp', 'seq'))  39.6 us
    all_gather x2, blocking collectives, on_device(): lax.all_gather(conv_kernel[layer_index], 'dp', axis=1, tiled=True)  37.6 us
  transfers between devices with their start and end apart: 49, of which 33 were waited for; matrix products, arithmetic and copies ran while one was open for 38% of the time, Pallas kernels for 0%

commit v1 on v0

--- a/solution.py
+++ b/solution.py
@@ -5,6 +5,18 @@
 
 EPSILON = 1e-05
 HIGHEST = lax.Precision.HIGHEST
+
+
+def doubled_up(value, axis, dim):
+    ways, here, turn = (lax.axis_size(axis), lax.axis_index(axis), value.shape[dim])
+    line, have = (value, 1)
+    while have < ways:
+        line = jnp.concatenate(
+            [line, lax.ppermute(line, axis, [(d, (d - have) % ways) for d in range(ways)])],
+            axis=dim,
+        )
+        have = 2 * have
+    return jnp.roll(line, here * turn, axis=dim)
 
 
 def from_behind(value, axis, steps):
@@ -287,7 +299,7 @@
             lax.all_gather(gate_weight[layer_index], "dp", axis=0, tiled=True),
             lax.all_gather(mix_weight[layer_index], "dp", axis=0, tiled=True),
             lax.all_gather(step_weight[layer_index], "dp", axis=0, tiled=True),
-            lax.all_gather(conv_kernel[layer_index], "dp", axis=1, tiled=True),
+            doubled_up(conv_kernel[layer_index], "dp", 1),
             lax.all_gather(conv_bias[layer_index], "dp", axis=0, tiled=True),
             lax.all_gather(gated_gain[layer_index], "dp", axis=0, tiled=True),
             lax.all_gather(out_weight[layer_index], "dp", axis=0, tiled=True),

time: 1360 us -> 1380 us (1.015)
  waiting for transfers between devices: 424 us -> 439 us
    slice x1 -> x3, local copies, waits for them, and re-layouts: 0.16 us -> 76.2 us  [the longest x2 76.1 us: layer_backward(): conv_kernel[0] * padded_grad[:, taps - 1:taps - 1 + group + taps - 1, :]]
    slice x2, local copies, waits for them, and re-layouts: 75.7 us -> 0.74 us  [layer_forward(): conv_kernel[tap_index] * extended[:, tap_index:tap_index + group, :]]
    all_gather x2, blocking collectives: 22.4 us -> 38.5 us  [on_device(): lax.all_gather(step_weight[layer_index], 'dp', axis=0, tiled=True)]
  transfers between devices with their start and end apart: 49 -> 53, of which waited for: 33 -> 34; matrix products, arithmetic and copies ran while one was open for 38% -> 37% of each run, Pallas kernels for 0% -> 0%
where the time goes in v1:
time: 1380 us; the launch traced here: 1370 us
  waiting for transfers between devices  439 us (32%)
  matrix products  247 us (18%)
  blocking collectives  193 us (14%)
  local copies, waits for them, and re-layouts  188 us (14%)
  starting transfers between devices  174 us (13%)
  other arithmetic  110 us (8%)
  between operations  20.7 us (2%)
    ppermute x32, waiting for transfers between devices, from_behind(): lax.ppermute(value, axis, [(source, source + steps) for source in range(f...  217 us
    ppermute x32, starting transfers between devices, from_behind(): lax.ppermute(value, axis, [(source, source + steps) for source in range(f...  167 us
    dot_general x22, matrix products, matmul(): return jnp.dot(left, right, precision=HIGHEST)  136 us
    psum x1, waiting for transfers between devices, on_device(): lax.psum((reduced[0], reduced[1], reduced[2], reduced[3], reduced[4], red...  128 us
    slice x2, local copies, waits for them, and re-layouts, layer_backward(): conv_kernel[0] * padded_grad[:, taps - 1:taps - 1 + group + taps - 1, :]  76.1 us
    reduce_scatter x2, waiting for transfers between devices, on_device(): lax.psum_scatter(weight_grads[2], 'dp', scatter_dimension=0, tiled=True)  52.1 us
    psum x1, blocking collectives, on_device(): skip_total = lax.psum(skip_grad, ('dp', 'seq'))  39.6 us
    all_gather x2, blocking collectives, on_device(): lax.all_gather(step_weight[layer_index], 'dp', axis=0, tiled=True)  38.5 us
  transfers between devices with their start and end apart: 53, of which 34 were waited for; matrix products, arithmetic and copies ran while one was open for 37% of the time, Pallas kernels for 0%

profile of v1, /device:TPU:0, one launch (start us, length us, event | category | flops | bytes accessed | tf_op | source)
XLA Modules:
  0.0 1371.5 jit_solution(9845379378460673194)
XLA Ops:
  24.2 26.1 %all-gather.3 = f32[1,768,24]{2,0,1:T(1,128)S(1)} all-gather(f32[1,192,24]{2,0,1:T(1,128)S(1)} %copy.601), channel_id=5, replica_groups=mesh['dp'=4,'seq'=8] {'dp'}, dimensions={1}, use_global_device_ids=true | all-gather | bytes 92160 | tf_op jit(solution)/shard_map/all_gather | solution.py:301
  55.0 18.8 %all-reduce.18 = (f32[768]{0:T(1024)S(1)}, f32[1792]{0:T(1024)}, f32[768]{0:T(1024)S(1)}, f32[1792]{0:T(1024)}) all-reduce(f32[768]{0:T(1024)S(1)} %dynamic-update-slice.1, f32[1792]{0:T(1024)S(1)} %dynamic-update-slice, f32[768]{0:T(1024)S(1)} %dynamic-update-slice.3, ...), channel_id=3, replica_groups=mesh['dp'=4,'seq'=8] {'dp'}, use_global_device_ids=true, to_apply=%add.5 | all-reduce | flops 5120 | bytes 40960 | tf_op jit(solution)/shard_map/all_gather | solution.py:298
  104.9 12.3 all-gather.10
  142.9 86.7 %while.40 = (s32[]{:T(128)}, f32[1,24,64,128]{3,2,1,0:T(8,128)S(1)}, f32[1,24]{1,0:T(1,128)S(1)}, f32[1,24,64,128]{3,2,1,0:T(8,128)S(1)}, s32[]{:T(128)}) while((s32[]{:T(128)}, f32[1,24,64,128]{3,2,1,0:T(8,128)S(1)}, f32[1,24]{1,0:T(1,128)S(1)}, f32[1,24,64,128]{3,2,1,0:T(8,128)S(1)}, s32[]{:T(128)}) %tuple.142), condition=%wide.region_4.6_spmd, body=%wide.region_3.5_spmd.sunk | while | flops 393218 | bytes 5505221 | solution.py:41
  263.9 12.3 all-gather.29.cloned.1.call-done
  318.3 100.2 %while.41 = (s32[]{:T(128)}, f32[1,24,64,128]{3,2,1,0:T(8,128)S(1)}, f32[1,24]{1,0:T(1,128)}, f32[1,24,64,128]{3,2,1,0:T(8,128)}, s32[]{:T(128)}) while((s32[]{:T(128)}, f32[1,24,64,128]{3,2,1,0:T(8,128)S(1)}, f32[1,24]{1,0:T(1,128)}, f32[1,24,64,128]{3,2,1,0:T(8,128)}, s32[]{:T(128)}) %tuple.145), condition=%wide.region_10.12_spmd, body=%wide.region_9.11_spmd.sunk | while | flops 393218 | bytes 5505221 | solution.py:41
  472.7 38.3 %slice_reduce_fusion.7 = (f32[1792]{0:T(1024)}, f32[1792]{0:T(1024)}, f32[1792]{0:T(1024)}, f32[1792]{0:T(1024)}) fusion(f32[1,4,1792]{1,0,2:T(1,128)S(1)} %all-gather.14), kind=kLoop, calls=%fused_computation.195 | loop fusion | bytes 57344 | tf_op jit(solution)/shard_map/slice | solution.py:232
  532.5 118.4 %while.42 = (s32[]{:T(128)}, f32[1,24,64,128]{3,2,1,0:T(8,128)}, f32[1,24]{1,0:T(1,128)}, f32[1,24,64,128]{3,2,1,0:T(8,128)}, s32[]{:T(128)}) while((s32[]{:T(128)}, f32[1,24,64,128]{3,2,1,0:T(8,128)}, f32[1,24]{1,0:T(1,128)}, f32[1,24,64,128]{3,2,1,0:T(8,128)}, s32[]{:T(128)}) %tuple.190), condition=%wide.region_14.16_spmd, body=%wide.region_13.15_spmd.sunk | while | flops 393218 | bytes 5505221 | solution.py:49
  551.4 18.8 %collective-permute-done.2 = f32[1,24,64,128]{3,2,1,0:T(8,128)} collective-permute-done((f32[1,24,64,128]{3,2,1,0:T(8,128)}, f32[1,24,64,128]{3,2,1,0:T(8,128)}, u32[]{:S(2)}, u32[]{:S(2)}) %collective-permute-start.2) | collective-permute-done | bytes 786464 | tf_op jit(solution)/shard_map/while/body/eval_jaxpr/ppermute | solution.py:25
  573.9 12.6 collective-permute-done.2
  622.6 12.3 collective-permute-done.2
  772.8 20.0 %all-gather.15 = f32[1,4,1792]{1,0,2:T(1,128)S(1)} all-gather(f32[1,4,448]{1,0,2:T(1,128)S(1)} %copy-done.53), channel_id=17, replica_groups=mesh['dp'=4,'seq'=8] {'dp'}, dimensions={2}, use_global_device_ids=true | all-gather | bytes 35840 | tf_op jit(solution)/shard_map/all_gather | solution.py:321
  792.7 37.7 %slice_reduce_fusion.3 = (f32[1792]{0:T(1024)S(1)}, f32[1792]{0:T(1024)S(1)}, f32[1792]{0:T(1024)S(1)}, f32[1792]{0:T(1024)S(1)}) fusion(f32[1,4,1792]{1,0,2:T(1,128)S(1)} %all-gather.15), kind=kLoop, calls=%fused_computation.191 | loop fusion | bytes 57344 | tf_op jit(solution)/shard_map/slice | solution.py:232
  845.4 111.2 %while.43 = (s32[]{:T(128)}, f32[1,24,64,128]{3,2,1,0:T(8,128)S(1)}, f32[1,24]{1,0:T(1,128)S(1)}, f32[1,24,64,128]{3,2,1,0:T(8,128)}, s32[]{:T(128)}) while((s32[]{:T(128)}, f32[1,24,64,128]{3,2,1,0:T(8,128)S(1)}, f32[1,24]{1,0:T(1,128)S(1)}, f32[1,24,64,128]{3,2,1,0:T(8,128)}, s32[]{:T(128)}) %tuple.189), condition=%wide.region_28.30_spmd, body=%wide.region_27.29_spmd.sunk | while | flops 393218 | bytes 5505221 | solution.py:49
  863.1 13.9 %collective-permute-done.3 = f32[1,24,64,128]{3,2,1,0:T(8,128)S(1)} collective-permute-done((f32[1,24,64,128]{3,2,1,0:T(8,128)}, f32[1,24,64,128]{3,2,1,0:T(8,128)S(1)}, u32[]{:S(2)}, u32[]{:S(2)}) %collective-permute-start.3) | collective-permute-done | bytes 786464 | tf_op jit(solution)/shard_map/while/body/eval_jaxpr/ppermute | solution.py:25
  896.0 12.7 collective-permute-done.3
  912.1 12.6 collective-permute-done.3
  944.0 12.6 collective-permute-done.3
  1025.6 52.1 %reduce-scatter.23.cloned.1.call-done = f32[192,1792]{1,0:T(8,128)} async-done(((f32[768,1792]{1,0:T(8,128)}), f32[192,1792]{1,0:T(8,128)}) %reduce-scatter.23.cloned.1.call-update) | async-done | bytes 1376272 | tf_op jit(solution)/shard_map/reduce_scatter | solution.py:337
  1087.5 39.6 %all-reduce.14 = (f32[1,24]{1,0:T(1,128)S(1)}, f32[1,24]{1,0:T(1,128)S(1)}) all-reduce(f32[1,24]{1,0:T(1,128)S(1)} %bitcast.669, f32[1,24]{1,0:T(1,128)S(1)} %bitcast.670), channel_id=1, replica_groups=mesh['dp'=4,'seq'=8] {'dp','seq'}, use_global_device_ids=true, to_apply=%region_91.93 | all-reduce | flops 48 | bytes 384 | tf_op jit(solution)/shard_map/psum | solution.py:357
  1143.4 17.5 %all-reduce.17 = (f32[768]{0:T(1024)S(1)}, f32[768]{0:T(1024)S(1)}, f32[1792]{0:T(1024)S(1)}, f32[1792]{0:T(1024)S(1)}, f32[1536]{0:T(1024)S(1)}, /*index=5*/f32[1536]{0:T(1024)S(1)}) all-reduce(f32[768]{0:T(1024)S(1)} %copy-done.140, f32[768]{0:T(1024)S(1)} %get-tuple-element.130, ...), channel_id=19, replica_groups=mesh['dp'=4,'seq'=8] {'dp'}, use_global_device_ids=true, to_apply=%region_44.46.clone | all-reduce | flops 8192 | bytes 65536
  1167.0 26.1 %reduce-scatter.31.cloned.1.call-done = f32[192,24]{1,0:T(8,128)} async-done(((f32[768,24]{1,0:T(8,128)}), f32[192,24]{1,0:T(8,128)}) %reduce-scatter.31.cloned.1.call-update) | async-done | bytes 18448
  1194.0 31.6 %all-reduce.15 = (f32[1,192]{1,0:T(1,128)S(1)}, f32[1,192]{1,0:T(1,128)S(1)}, f32[1,192,24]{1,2,0:T(8,128)S(1)}, f32[1,192,24]{1,2,0:T(8,128)S(1)}, f32[1,4,448]...) all-reduce(f32[1,192]{1,0:T(1,128)S(1)} %bitcast.661, ...), channel_id=1, replica_groups=mesh['dp'=4,'seq'=8] {'seq'}, use_global_device_ids=true, to_apply=%region_45.47 | all-reduce | flops 14848 | bytes 118784 | tf_op jit(solution)/shard_map/psum | solution.py:344
  1228.6 128.5 %all-reduce.21.cloned.1.call-done = (f32[1,192,1536]{2,1,0:T(8,128)}, f32[1,192,1536]{2,1,0:T(8,128)}, f32[1,192,1792]{2,1,0:T(8,128)}, f32[1,192,1792]{2,1,0:T(...) async-done(((f32[1,192,1536]{2,1,0:T(8,128)}, f32[1,192,1536]{2,1,0:T(8,128)}, f32[1,192,1792]{2,1,0:T(8,128)}, f32[1,192,1792]{2,1,0:T(8,128)}, ...) | async-done | bytes 7471120 | tf_op jit(solution)/shard_map/psum | solution.py:344
  (747 shorter events, 793.7 us)
Async XLA Ops:
  7.2 111.2 %all-gather.23.cloned.1.call-start = ((), (), s32[]{:S(2)}) async-start(), calls=%async_computation.16 | async-start | bytes 6881280 | tf_op jit(solution)/shard_map/all_gather | solution.py:300
  10.7 232.9 %all-gather.25.cloned.1.call-start = ((), (), s32[]{:S(2)}) async-start(), calls=%async_computation.17 | async-start | bytes 5898240 | tf_op jit(solution)/shard_map/all_gather | solution.py:299
  14.0 240.4 %all-gather.27.cloned.1.call-start = ((), (), s32[]{:S(2)}) async-start(), calls=%async_computation.18 | async-start | bytes 5898240 | tf_op jit(solution)/shard_map/all_gather | solution.py:305
  17.2 259.0 %all-gather.29.cloned.1.call-start = ((), (), s32[]{:S(2)}) async-start(), calls=%async_computation.19 | async-start | bytes 6881280 | tf_op jit(solution)/shard_map/all_gather | solution.py:300
  17.8 414.6 %all-gather.31.cloned.1.call-start = ((), (), s32[]{:S(2)}) async-start(), calls=%async_computation.20 | async-start | bytes 5898240 | tf_op jit(solution)/shard_map/all_gather | solution.py:299
  18.5 424.1 %all-gather.33.cloned.1.call-start = ((), (), s32[]{:S(2)}) async-start(), calls=%async_computation.21 | async-start | bytes 5898240 | tf_op jit(solution)/shard_map/all_gather | solution.py:305
  18.7 79.6 %collective-permute-start.7 = (f32[4,448]{0,1:T(8,128)S(1)}, f32[4,448]{0,1:T(8,128)}, u32[]{:S(2)}, u32[]{:S(2)}) collective-permute-start(f32[4,448]{0,1:T(8,128)S(1)} %bitcast.629), channel_id=1, source_target_pairs={{0,24},{8,0},{16,8},{24,16},{1,25},{9,1},{17,9},{25,17},{2,26},{10... | collective-permute-start | bytes 21512 | tf_op jit(solution)/shard_map/ppermute | solution.py:15
  22.8 77.3 %collective-permute-start.4 = (f32[4,448]{0,1:T(8,128)S(1)}, f32[4,448]{0,1:T(8,128)}, u32[]{:S(2)}, u32[]{:S(2)}) collective-permute-start(f32[4,448]{0,1:T(8,128)S(1)} %bitcast.627), channel_id=1, source_target_pairs={{0,24},{8,0},{16,8},{24,16},{1,25},{9,1},{17,9},{25,17},{2,26},{10... | collective-permute-start | bytes 21512 | tf_op jit(solution)/shard_map/ppermute | solution.py:15
  23.4 1002.1 %reduce-scatter.21.cloned.1.call-start = ((), (), s32[]{:S(2)}) async-start(), calls=%async_computation.11 | async-start | bytes 5898240 | tf_op jit(solution)/shard_map/reduce_scatter | solution.py:336
  99.4 17.8 %collective-permute-start.8 = (f32[4,896]{1,0:T(4,128)S(1)}, f32[4,896]{1,0:T(4,128)S(1)}, u32[]{:S(2)}, u32[]{:S(2)}) collective-permute-start(f32[4,896]{1,0:T(4,128)S(1)} %pad_maximum_fusion.16), channel_id=1, source_target_pairs={{0,16},{8,24},{16,0},{24,8},{1,17},{9,25},{17,1},{25,9},{2,18},{10... | collective-permute-start | bytes 43016 | tf_op jit(solution)/shard_map/ppermute | solution.py:15
  101.2 16.8 %collective-permute-start.5 = (f32[4,896]{1,0:T(4,128)S(1)}, f32[4,896]{1,0:T(4,128)S(1)}, u32[]{:S(2)}, u32[]{:S(2)}) collective-permute-start(f32[4,896]{1,0:T(4,128)S(1)} %pad_maximum_fusion.15), channel_id=1, source_target_pairs={{0,16},{8,24},{16,0},{24,8},{1,17},{9,25},{17,1},{25,9},{2,18},{10... | collective-permute-start | bytes 43016 | tf_op jit(solution)/shard_map/ppermute | solution.py:15
  461.0 564.6 %reduce-scatter.29.cloned.1.call-start = ((), (), s32[]{:S(2)}) async-start(), calls=%async_computation.15 | async-start | bytes 5898240 | tf_op jit(solution)/shard_map/reduce_scatter | solution.py:342
  531.5 494.1 %reduce-scatter.19.cloned.1.call-start = ((), (), s32[]{:S(2)}) async-start(), calls=%async_computation.10 | async-start | bytes 5898240 | tf_op jit(solution)/shard_map/reduce_scatter | solution.py:336
  550.2 20.1 %collective-permute-start.2 = (f32[1,24,64,128]{3,2,1,0:T(8,128)}, f32[1,24,64,128]{3,2,1,0:T(8,128)}, u32[]{:S(2)}, u32[]{:S(2)}) collective-permute-start(f32[1,24,64,128]{3,2,1,0:T(8,128)} %multiply_add_fusion.12), channel_id=1, source_target_pairs={{1,0},{2,1},{3,2},{4,3},{5,4},{6,5},{7,6},{9,8},{10,9},{11,10},{12... | collective-permute-start | bytes 2359304 | tf_op jit(solution)/shard_map/while/body/eval_jaxpr/ppermute | solution.py:25
  701.2 23.4 %collective-permute-start.10 = (f32[1,3,1792]{2,1,0:T(4,128)}, f32[1,3,1792]{2,1,0:T(4,128)}, u32[]{:S(2)}, u32[]{:S(2)}) collective-permute-start(f32[1,3,1792]{2,1,0:T(4,128)} %slice.390), channel_id=1, source_target_pairs={{1,0},{2,1},{3,2},{4,3},{5,4},{6,5},{7,6},{9,8},{10,9},{11,10},{12... | collective-permute-start | bytes 64520 | tf_op jit(solution)/shard_map/ppermute | solution.py:25
  751.3 274.3 %reduce-scatter.27.cloned.1.call-start = ((), (), s32[]{:S(2)}) async-start(), calls=%async_computation.14 | async-start | bytes 5898240 | tf_op jit(solution)/shard_map/reduce_scatter | solution.py:342
  759.0 266.7 %reduce-scatter.25.cloned.1.call-start = ((), (), s32[]{:S(2)}) async-start(), calls=%async_computation.13 | async-start | bytes 6881280 | tf_op jit(solution)/shard_map/reduce_scatter | solution.py:337
  767.7 310.0 %reduce-scatter.23.cloned.1.call-start = ((), (), s32[]{:S(2)}) async-start(), calls=%async_computation.12 | async-start | bytes 6881280 | tf_op jit(solution)/shard_map/reduce_scatter | solution.py:337
  861.8 15.2 %collective-permute-start.3 = (f32[1,24,64,128]{3,2,1,0:T(8,128)}, f32[1,24,64,128]{3,2,1,0:T(8,128)S(1)}, u32[]{:S(2)}, u32[]{:S(2)}) collective-permute-start(f32[1,24,64,128]{3,2,1,0:T(8,128)} %multiply_add_fusion.13), channel_id=1, source_target_pairs={{1,0},{2,1},{3,2},{4,3},{5,4},{6,5},{7,6},{9,8},{10,9},{11,10},{12... | collective-permute-start | bytes 2359304 | tf_op jit(solution)/shard_map/while/body/eval_jaxpr/ppermute | solution.py:25
  1012.4 150.1 %reduce-scatter.37.cloned.1.call-start = ((), (), s32[]{:S(2)}) async-start(), calls=%async_computation.25 | async-start | bytes 1146880
  1014.5 149.1 %reduce-scatter.35.cloned.1.call-start = ((), (), s32[]{:S(2)}) async-start(), calls=%async_computation.24 | async-start | bytes 1146880
  1015.9 150.1 %reduce-scatter.33.cloned.1.call-start = ((), (), s32[]{:S(2)}) async-start(), calls=%async_computation.23 | async-start | bytes 491520
  1018.2 174.8 %reduce-scatter.31.cloned.1.call-start = ((), (), s32[]{:S(2)}) async-start(), calls=%async_computation.22 | async-start | bytes 491520
  1025.4 331.7 %all-reduce.21.cloned.1.call-start = ((), (), s32[]{:S(2)}) async-start(), calls=%async_computation.26 | async-start | bytes 14942208 | tf_op jit(solution)/shard_map/psum | solution.py:344
  (199 other events, 2225.9 us)
Sparse Core Ops, SparseCore 0:
  10.8 79.9 all-gather.22
  92.7 59.2 all-gather.24
  153.8 57.0 all-gather.26
  212.6 63.6 all-gather.28
  277.9 57.0 all-gather.30
  336.7 57.0 all-gather.32
  461.1 69.9 reduce-scatter.20
  534.0 69.7 reduce-scatter.28
  751.4 74.4 reduce-scatter.18
  828.7 57.0 reduce-scatter.26
  888.9 63.6 reduce-scatter.24
  1012.5 65.1 reduce-scatter.22
  1081.2 27.1 reduce-scatter.36
  1111.8 27.0 reduce-scatter.34
  1141.5 24.5 reduce-scatter.32
  1168.7 24.3 reduce-scatter.30
  1195.8 161.2 all-reduce.20
